TPU v7x, 256 devices: a whole 4x4x8 slice. The times are simulated.
256 devices in a mesh: view: 8 (over y, x_lo), band: 32 (over x_hi, z, core).
Axes of the slice: x: 4 (x_hi: 2, x_lo: 2; x = x_hi * 2 + x_lo), y: 4, z: 8, core: 2. Of those that a mesh axis runs over, the one named last changes fastest.
Arguments:
- features: float32 [8, 256, 512, 128], P('view', 'band'), may hold values from -6 to 6
- tempers: float32 [8, 256, 512], P('view', 'band'), may hold values from 0.5 to 80
- partners: int32 [8, 2], replicated, may hold values from 0 to 7, as said below
- conv_one: bfloat16 [3, 3, 128, 128], replicated, may hold values from -0.1875 to 0.1875
- conv_two: bfloat16 [3, 3, 128, 128], replicated, may hold values from -0.1875 to 0.1875
- query_weight: bfloat16 [128, 128], replicated, may hold values from -0.5 to 0.5
- key_weight: bfloat16 [128, 128], replicated, may hold values from -0.5 to 0.5
- value_weight: bfloat16 [128, 128], replicated, may hold values from -0.5 to 0.5
- out_weight: bfloat16 [128, 128], replicated, may hold values from -0.5 to 0.5
- norm_gain: float32 [128], replicated, may hold values from 0.25 to 1.75
- message_gain: float32 [128], replicated, may hold values from 0.25 to 1.75
Outputs:
- refined: float32 [8, 256, 512, 128], P('view', 'band')
Inputs may be any that keep to these rules, and one draw needn't show every extreme that they name: Column 0 and column 1 are each a permutation of the 8 views; a view is never its own partner, and its two partners differ. At least one view has as its first partner the view 4 positions away from it (modulo 8).
All inputs are finite; a program needn't handle non-finite values.
Results may differ from a plain program's by a relative error of at most 0.0065.
Values may be sent and summed in bfloat16 or wider, within the bound.
A program may use at most 64 MiB of HBM per device.

v0:
```python
import math
import jax
import jax.numpy as jnp
from jax import lax
from jax.sharding import PartitionSpec as P

epsilon = 1e-06


def extended(cells, sides, width):
    for axis, dim in sides:
        count = lax.axis_size(axis)
        ends = count - 1
        head = lax.slice_in_dim(cells, 0, width, axis=dim)
        tail = lax.slice_in_dim(cells, cells.shape[dim] - width, cells.shape[dim], axis=dim)
        cells = jnp.concatenate(
            [
                lax.ppermute(tail, axis, [(i, (i + 1) % count) for i in range(ends)]),
                cells,
                lax.ppermute(head, axis, [((i + 1) % count, i) for i in range(ends)]),
            ],
            axis=dim,
        )
    return cells


def root_norm(values, gain):
    mean_square = jnp.mean(values * values, axis=-1, keepdims=True)
    return values * lax.rsqrt(mean_square + epsilon) * gain


def convolve(padded, kernel):
    leading = padded.shape[:-3]
    out_rows = padded.shape[-3] - 2
    columns = padded.shape[-2]
    channels = padded.shape[-1]
    widened = jnp.pad(padded, [(0, 0)] * len(leading) + [(0, 0), (1, 1), (0, 0)])
    summed = jnp.zeros(leading + (out_rows, columns, kernel.shape[-1]), jnp.float32)
    for row_tap in range(3):
        for col_tap in range(3):
            window = widened[..., row_tap : row_tap + out_rows, col_tap : col_tap + columns, :]
            product = jnp.dot(
                window.reshape(-1, channels),
                kernel[row_tap, col_tap],
                preferred_element_type=jnp.float32,
            )
            summed = summed + product.reshape(summed.shape)
    return summed


def route_pair(normed_rows, own_view, partners):
    every_view = lax.all_gather(normed_rows[None], "view", axis=0, tiled=True)
    chosen = lax.dynamic_index_in_dim(partners, own_view, 0, keepdims=False)
    return jnp.take(every_view, chosen, axis=0)


def per_device(
    features,
    tempers,
    partners,
    conv_one,
    conv_two,
    query_weight,
    key_weight,
    value_weight,
    out_weight,
    norm_gain,
    message_gain,
):
    current = features[0]
    temper = tempers[0]
    row_count, columns, channels = current.shape
    first_input = jax.nn.silu(current).astype(jnp.bfloat16)
    first_rows = extended(first_input, (("band", 0),), 1)
    state_one = current + convolve(first_rows, conv_one)
    second_input = jax.nn.silu(state_one).astype(jnp.bfloat16)
    second_rows = extended(second_input, (("band", 0),), 1)
    state_two = state_one + convolve(second_rows, conv_two)
    normed = root_norm(state_two, norm_gain).astype(jnp.bfloat16)
    flat_normed = normed.reshape(-1, channels)
    queries = (
        jnp.dot(flat_normed, query_weight, preferred_element_type=jnp.float32)
        .astype(jnp.bfloat16)
        .reshape(normed.shape)
    )
    own_view = lax.axis_index("view")
    paired = route_pair(normed, own_view, partners)
    paired_rows = extended(paired, (("band", 1),), 1)
    pair_flat = paired_rows.reshape(-1, channels)
    key_rows = (
        jnp.dot(pair_flat, key_weight, preferred_element_type=jnp.float32)
        .astype(jnp.bfloat16)
        .reshape(paired_rows.shape)
    )
    value_rows = (
        jnp.dot(pair_flat, value_weight, preferred_element_type=jnp.float32)
        .astype(jnp.bfloat16)
        .reshape(paired_rows.shape)
    )
    block_size = min(columns, 512)
    factor = 1.0 / math.sqrt(channels)

    def attend_row(row_index):
        query_row = lax.dynamic_index_in_dim(queries, row_index, 0, keepdims=False)
        temper_row = lax.dynamic_index_in_dim(temper, row_index, 0, keepdims=False) * factor
        key_window = lax.dynamic_slice_in_dim(key_rows, row_index, 3, 1).reshape(
            2, 3 * columns, channels
        )
        value_window = lax.dynamic_slice_in_dim(value_rows, row_index, 3, 1).reshape(
            2, 3 * columns, channels
        )
        summed = jnp.zeros((columns, channels), jnp.float32)
        for partner in range(2):
            scores = lax.dot_general(
                query_row,
                key_window[partner],
                (((1,), (1,)), ((), ())),
                preferred_element_type=jnp.float32,
            )
            scores = scores * temper_row[0:block_size, None]
            row_peak = jnp.max(scores, axis=-1, keepdims=True)
            lifted = jnp.exp(scores - row_peak)
            shares = (lifted / jnp.sum(lifted, axis=-1, keepdims=True)).astype(jnp.bfloat16)
            pieces = [
                jnp.dot(shares, value_window[partner], preferred_element_type=jnp.float32).astype(
                    jnp.bfloat16
                )
            ]
            blended = jnp.concatenate(pieces, axis=0)
            summed = summed + jnp.dot(blended, out_weight, preferred_element_type=jnp.float32)
        return summed

    messages = lax.map(attend_row, jnp.arange(row_count, dtype=jnp.int32))
    refined = state_two + root_norm(messages, message_gain)
    return refined[None]


def solution(mesh):
    in_specs = (
        P("view", "band", None, None),
        P("view", "band", None),
        P(),
        P(),
        P(),
        P(),
        P(),
        P(),
        P(),
        P(),
        P(),
    )
    out_specs = P("view", "band", None, None)
    return jax.shard_map(
        per_device, mesh=mesh, in_specs=in_specs, out_specs=out_specs, check_vma=False
    )
```

profile of v0, /device:TPU:6, one launch (start us, length us, event | category | flops | bytes accessed | tf_op | source)
XLA Modules:
  0.0 379.8 jit_solution(6802062921291044743)
XLA Ops:
  6.5 2.3 fusion.19
  8.9 1.9 collective-permute-start
  10.8 8.0 %collective-permute-start.1 = (bf16[1,512,128]{2,1,0:T(8,128)(2,1)S(1)}, bf16[1,512,128]{2,1,0:T(8,128)(2,1)S(1)}, u32[]{:S(2)}, u32[]{:S(2)}) collective-permute-start(bf16[1,512,128]{2,1,0:T(8,128)(2,1)S(1)} %get-tuple-element.79), channel_id=1, source_target_pairs={{1,0},{2,1},{3,2},{4,3},{5,4},{6,5},{7,6},{8,7},{9,8},{10,9},{11,1... | collective-permute-start | bytes 393224 | tf_op jit(solution)/shard_map/ppermute | solution.py:20
  19.6 1.8 collective-permute-done.1
  24.7 1.5 multiply_convert_fusion.1
  26.2 1.9 collective-permute-start.2
  28.2 7.4 %collective-permute-start.3 = (bf16[1,512,128]{2,1,0:T(8,128)(2,1)S(1)}, bf16[1,512,128]{2,1,0:T(8,128)(2,1)S(1)}, u32[]{:S(2)}, u32[]{:S(2)}) collective-permute-start(bf16[1,512,128]{2,1,0:T(8,128)(2,1)S(1)} %get-tuple-element.77), channel_id=1, source_target_pairs={{1,0},{2,1},{3,2},{4,3},{5,4},{6,5},{7,6},{8,7},{9,8},{10,9},{11,1... | collective-permute-start | bytes 393224 | tf_op jit(solution)/shard_map/ppermute | solution.py:20
  36.3 1.8 collective-permute-done.3
  41.4 1.3 multiply_reduce_fusion.1
  42.7 1.3 copy-done.2
  44.0 1.5 multiply_convert_fusion
  45.8 169.9 %all-gather.3.cloned.1.call-done = bf16[64,512,128]{2,1,0:T(8,128)(2,1)} async-done(((bf16[8,512,128]{2,1,0:T(8,128)(2,1)}), bf16[64,512,128]{2,1,0:T(8,128)(2,1)}) %all-gather.3.cloned.1.call-update) | async-done | bytes 8388624 | tf_op jit(solution)/shard_map/all_gather | solution.py:52
  215.7 4.3 %gather_fusion = bf16[2,8,512,128]{3,2,1,0:T(8,128)(2,1)S(1)} fusion(bf16[8,8,512,128]{3,2,1,0:T(8,128)(2,1)} %bitcast.194, s32[1024]{0:T(1024)S(1)} %pad_clamp_fusion), kind=kCustom, calls=%fused_computation | custom fusion | bytes 4194312 | tf_op jit(solution)/shard_map/jit(_take)/gather | solution.py:54
  220.4 1.9 collective-permute-start.4
  222.3 7.4 %collective-permute-start.5 = (bf16[2,1,512,128]{3,2,1,0:T(8,128)(2,1)S(1)}, bf16[2,1,512,128]{3,2,1,0:T(8,128)(2,1)S(1)}, u32[]{:S(2)}, u32[]{:S(2)}) collective-permute-start(bf16[2,1,512,128]{3,2,1,0:T(8,128)(2,1)S(1)} %get-tuple-element.75), channel_id=1, source_target_pairs={{1,0},{2,1},{3,2},{4,3},{5,4},{6,5},{7,6},{8,7},{9,8},{10,9},{11,1... | collective-permute-start | bytes 786440 | tf_op jit(solution)/shard_map/ppermute | solution.py:20
  229.8 1.4 convolution_convert_fusion.2
  231.7 1.8 collective-permute-done.5
  233.8 2.3 convolution_convert_fusion
  236.1 2.3 convolution_convert_fusion.1
  238.5 129.1 %while.10 = (s32[]{:T(128)}, f32[8,512,128]{2,1,0:T(8,128)}, s32[8]{0:T(128)S(1)}, bf16[8,512,128]{2,1,0:T(8,128)(2,1)}, bf16[2,10,512,128]{3,2,1,0:T(8,128)(2,1...) while((s32[]{:T(128)}, f32[8,512,128]{2,1,0:T(8,128)}, ...), condition=%wide.region_6.7_spmd, body=%wide.region_1.0_spmd.sunk | while | flops 850065920 | bytes 26308876 | solution.py:133
  241.8 0.7 dynamic-slice_multiply_fusion.2
  242.5 2.4 constant_dynamic-slice_fusion.5
  244.9 1.6 fusion.146
  247.0 2.6 fusion.148
  249.6 1.6 fusion.149
  252.1 2.5 fusion.151
  257.9 0.7 dynamic-slice_multiply_fusion.2
  258.7 2.4 constant_dynamic-slice_fusion.5
  261.0 1.6 fusion.146
  263.2 2.6 fusion.148
  265.7 1.6 fusion.149
  268.3 2.5 fusion.151
  274.8 2.4 constant_dynamic-slice_fusion.5
  277.2 1.6 fusion.146
  279.3 2.5 fusion.148
  281.9 1.6 fusion.149
  284.4 2.5 fusion.151
  291.0 2.4 constant_dynamic-slice_fusion.5
  293.3 1.6 fusion.146
  295.5 2.6 fusion.148
  298.0 1.6 fusion.149
  300.6 2.5 fusion.151
  307.1 2.4 constant_dynamic-slice_fusion.5
  309.5 1.6 fusion.146
  311.6 2.6 fusion.148
  314.2 1.6 fusion.149
  316.7 2.5 fusion.151
  323.2 2.4 constant_dynamic-slice_fusion.5
  325.6 1.6 fusion.146
  327.7 2.6 fusion.148
  330.3 1.6 fusion.149
  332.9 2.5 fusion.151
  339.4 2.4 constant_dynamic-slice_fusion.5
  341.7 1.6 fusion.146
  343.9 2.6 fusion.148
  346.4 1.6 fusion.149
  349.0 2.5 fusion.151
  355.5 2.4 constant_dynamic-slice_fusion.5
  357.9 1.6 fusion.146
  360.0 2.6 fusion.148
  362.5 1.6 fusion.149
  365.1 2.5 fusion.151
  367.6 2.4 multiply_reduce_fusion
  370.0 2.9 add_bitcast_fusion
  (107 shorter events, 30.8 us)
Async XLA Ops:
  6.5 227.2 %copy-start = (bf16[128,128]{1,0:T(8,128)(2,1)S(1)}, bf16[128,128]{1,0:T(8,128)(2,1)}, u32[]{:S(2)}) copy-start(bf16[128,128]{1,0:T(8,128)(2,1)} %param.20) | copy-start | bytes 98308
  6.5 12.3 %copy-start.6 = (f32[1,8,512,128]{3,2,1,0:T(8,128)S(1)}, f32[1,8,512,128]{3,2,1,0:T(8,128)}, u32[]{:S(2)}) copy-start(f32[1,8,512,128]{3,2,1,0:T(8,128)} %param.13) | copy-start | bytes 6291460
  6.5 12.3 %copy-start.8 = (bf16[3,3,128,128]{3,2,1,0:T(8,128)(2,1)S(1)}, bf16[3,3,128,128]{3,2,1,0:T(8,128)(2,1)}, u32[]{:S(2)}) copy-start(bf16[3,3,128,128]{3,2,1,0:T(8,128)(2,1)} %param.16) | copy-start | bytes 884740
  6.5 209.2 %all-gather.3.cloned.1.call-start = ((), (), s32[]{:S(2)}) async-start(), calls=%async_computation | async-start | bytes 9437184 | tf_op jit(solution)/shard_map/all_gather | solution.py:52
  8.9 10.7 %collective-permute-start = (bf16[1,512,128]{2,1,0:T(8,128)(2,1)S(1)}, bf16[1,512,128]{2,1,0:T(8,128)(2,1)S(1)}, u32[]{:S(2)}, u32[]{:S(2)}) collective-permute-start(bf16[1,512,128]{2,1,0:T(8,128)(2,1)S(1)} %get-tuple-element.78), channel_id=1, source_target_pairs={{0,1},{1,2},{2,3},{3,4},{4,5},{5,6},{6,7},{7,8},{8,9},{9,10},{10,1... | collective-permute-start | bytes 393224 | tf_op jit(solution)/shard_map/ppermute | solution.py:18
  10.8 10.6 %collective-permute-start.1 = (bf16[1,512,128]{2,1,0:T(8,128)(2,1)S(1)}, bf16[1,512,128]{2,1,0:T(8,128)(2,1)S(1)}, u32[]{:S(2)}, u32[]{:S(2)}) collective-permute-start(bf16[1,512,128]{2,1,0:T(8,128)(2,1)S(1)} %get-tuple-element.79), channel_id=1, source_target_pairs={{1,0},{2,1},{3,2},{4,3},{5,4},{6,5},{7,6},{8,7},{9,8},{10,9},{11,1... | collective-permute-start | bytes 393224 | tf_op jit(solution)/shard_map/ppermute | solution.py:20
  24.7 10.9 %copy-start.7 = (bf16[3,3,128,128]{3,2,1,0:T(8,128)(2,1)S(1)}, bf16[3,3,128,128]{3,2,1,0:T(8,128)(2,1)}, u32[]{:S(2)}) copy-start(bf16[3,3,128,128]{3,2,1,0:T(8,128)(2,1)} %param.17) | copy-start | bytes 884740
  26.2 10.0 %collective-permute-start.2 = (bf16[1,512,128]{2,1,0:T(8,128)(2,1)S(1)}, bf16[1,512,128]{2,1,0:T(8,128)(2,1)S(1)}, u32[]{:S(2)}, u32[]{:S(2)}) collective-permute-start(bf16[1,512,128]{2,1,0:T(8,128)(2,1)S(1)} %get-tuple-element.76), channel_id=1, source_target_pairs={{0,1},{1,2},{2,3},{3,4},{4,5},{5,6},{6,7},{7,8},{8,9},{9,10},{10,1... | collective-permute-start | bytes 393224 | tf_op jit(solution)/shard_map/ppermute | solution.py:18
  28.2 9.9 %collective-permute-start.3 = (bf16[1,512,128]{2,1,0:T(8,128)(2,1)S(1)}, bf16[1,512,128]{2,1,0:T(8,128)(2,1)S(1)}, u32[]{:S(2)}, u32[]{:S(2)}) collective-permute-start(bf16[1,512,128]{2,1,0:T(8,128)(2,1)S(1)} %get-tuple-element.77), channel_id=1, source_target_pairs={{1,0},{2,1},{3,2},{4,3},{5,4},{6,5},{7,6},{8,7},{9,8},{10,9},{11,1... | collective-permute-start | bytes 393224 | tf_op jit(solution)/shard_map/ppermute | solution.py:20
  41.4 2.6 copy-start.13
  42.7 1.3 copy-start.2
  44.0 1.6 copy-start.11
  220.1 9.7 %copy-start.5 = (bf16[8,512,128]{2,1,0:T(8,128)(2,1)S(1)}, bf16[8,512,128]{2,1,0:T(8,128)(2,1)}, u32[]{:S(2)}) copy-start(bf16[8,512,128]{2,1,0:T(8,128)(2,1)} %multiply_convert_fusion) | copy-start | bytes 3145732
  220.1 9.7 %copy-start.9 = (bf16[128,128]{1,0:T(8,128)(2,1)S(1)}, bf16[128,128]{1,0:T(8,128)(2,1)}, u32[]{:S(2)}) copy-start(bf16[128,128]{1,0:T(8,128)(2,1)} %param.18) | copy-start | bytes 98308
  220.4 11.3 %collective-permute-start.4 = (bf16[2,1,512,128]{3,2,1,0:T(8,128)(2,1)S(1)}, bf16[2,1,512,128]{3,2,1,0:T(8,128)(2,1)S(1)}, u32[]{:S(2)}, u32[]{:S(2)}) collective-permute-start(bf16[2,1,512,128]{3,2,1,0:T(8,128)(2,1)S(1)} %get-tuple-element.74), channel_id=1, source_target_pairs={{0,1},{1,2},{2,3},{3,4},{4,5},{5,6},{6,7},{7,8},{8,9},{9,10},{10,1... | collective-permute-start | bytes 786440 | tf_op jit(solution)/shard_map/ppermute | solution.py:18
  222.3 11.1 %collective-permute-start.5 = (bf16[2,1,512,128]{3,2,1,0:T(8,128)(2,1)S(1)}, bf16[2,1,512,128]{3,2,1,0:T(8,128)(2,1)S(1)}, u32[]{:S(2)}, u32[]{:S(2)}) collective-permute-start(bf16[2,1,512,128]{3,2,1,0:T(8,128)(2,1)S(1)} %get-tuple-element.75), channel_id=1, source_target_pairs={{1,0},{2,1},{3,2},{4,3},{5,4},{6,5},{7,6},{8,7},{9,8},{10,9},{11,1... | collective-permute-start | bytes 786440 | tf_op jit(solution)/shard_map/ppermute | solution.py:20
  233.8 2.4 copy-start.10
  251.1 1.0 copy-start.4
  267.3 1.0 copy-start.4
  283.4 1.0 copy-start.4
  299.6 1.0 copy-start.4
  315.7 1.0 copy-start.4
  331.9 1.0 copy-start.4
  348.0 1.0 copy-start.4
  364.1 1.0 copy-start.4
  367.6 2.4 copy-start.3
  367.6 2.4 copy-start.12
  370.0 3.0 copy-start.1
Sparse Core Ops, SparseCore 0:
  45.7 169.9 all-gather.2
where the time goes:
time: 382 us; the launch traced here: 380 us
  waiting for transfers between devices  176 us (46%)
  matrix products  81.6 us (21%)
  local copies, waits for them, and re-layouts  32.7 us (9%)
  starting transfers between devices  28.6 us (7%)
  other arithmetic  25.3 us (7%)
  loops' own time  21.9 us (6%)
  between operations  13.7 us (4%)
    all_gather x1, waiting for transfers between devices, route_pair(): every_view = lax.all_gather(normed_rows[None], 'view', axis=0, tiled=True)  170 us
    dot_general x16, matrix products, attend_row(): jnp.dot(blended, out_weight, preferred_element_type=jnp.float32)  40.5 us
    dot_general x16, matrix products, attend_row(): lax.dot_general(query_row, key_window[partner], (((1,), (1,)), ((), ())),...  25.1 us
    ppermute x3, starting transfers between devices, extended(): lax.ppermute(head, axis, [((i + 1) % count, i) for i in range(ends)])  22.9 us
    another operation x1, loops' own time, per_device(): messages = lax.map(attend_row, jnp.arange(row_count, dtype=jnp.int32))  21.9 us
    slice x8, local copies, waits for them, and re-layouts, attend_row(): value_window[partner]  18.9 us
    dot_general x18, matrix products, convolve(): jnp.dot(window.reshape(-1, channels), kernel[row_tap, col_tap], preferred...  9.82 us
    reduce_sum x16, other arithmetic, attend_row(): jnp.sum(lifted, axis=-1, keepdims=True)  9.08 us
  transfers between devices with their start and end apart: 7, of which 6 were waited for; matrix products, arithmetic and copies ran while one was open for 1% of the time, Pallas kernels for 0%

commit v1 on v0

--- a/solution.py
+++ b/solution.py
@@ -49,7 +49,9 @@
 
 
 def route_pair(normed_rows, own_view, partners):
-    every_view = lax.all_gather(normed_rows[None], "view", axis=0, tiled=True)
+    every_view = jnp.concatenate(
+        lax.all_to_all(jnp.stack([normed_rows[None]] * lax.axis_size("view")), "view", 0, 0), axis=0
+    )
     chosen = lax.dynamic_index_in_dim(partners, own_view, 0, keepdims=False)
     return jnp.take(every_view, chosen, axis=0)
 

time: 382 us -> 322 us (0.84)
  waiting for transfers between devices: 176 us -> 93.9 us
  local copies, waits for them, and re-layouts: 32.7 us -> 53.3 us
  between operations: 13.7 us -> 0.3 us
  starting transfers between devices: 28.6 us -> 35.8 us
  loops' own time: 21.9 us -> 27.1 us
    all_gather x1 -> x0, waiting for transfers between devices: 170 us -> none  [route_pair(): every_view = lax.all_gather(normed_rows[None], 'view', axis=0, tiled=True)]
    all_to_all x0 -> x1, waiting for transfers between devices: none -> 87.7 us  [route_pair(): lax.all_to_all(jnp.stack([normed_rows[None]] * lax.axis_size('view')), 'v...]
    while x16 -> x32, local copies, waits for them, and re-layouts: 3.45 us -> 16.5 us
    all_to_all x0 -> x1, starting transfers between devices: none -> 6.02 us  [route_pair(): lax.all_to_all(jnp.stack([normed_rows[None]] * lax.axis_size('view')), 'v...]
    another operation x0 -> x1, local copies, waits for them, and re-layouts: none -> 5.43 us  [route_pair(): jnp.stack([normed_rows[None]] * lax.axis_size('view'))]
    another operation x1, loops' own time: 21.9 us -> 27.1 us  [per_device(): messages = lax.map(attend_row, jnp.arange(row_count, dtype=jnp.int32))]
where the time goes in v1:
time: 322 us; the launch traced here: 320 us
  waiting for transfers between devices  93.9 us (29%)
  matrix products  84.8 us (26%)
  local copies, waits for them, and re-layouts  53.3 us (17%)
  starting transfers between devices  35.8 us (11%)
  loops' own time  27.1 us (8%)
  other arithmetic  24.5 us (8%)
    all_to_all x1, waiting for transfers between devices, route_pair(): lax.all_to_all(jnp.stack([normed_rows[None]] * lax.axis_size('view')), 'v...  87.7 us
    dot_general x16, matrix products, attend_row(): jnp.dot(blended, out_weight, preferred_element_type=jnp.float32)  42.5 us
    another operation x1, loops' own time, per_device(): messages = lax.map(attend_row, jnp.arange(row_count, dtype=jnp.int32))  27.1 us
    dot_general x16, matrix products, attend_row(): lax.dot_general(query_row, key_window[partner], (((1,), (1,)), ((), ())),...  26.5 us
    ppermute x3, starting transfers between devices, extended(): lax.ppermute(head, axis, [((i + 1) % count, i) for i in range(ends)])  24 us
    slice x8, local copies, waits for them, and re-layouts, attend_row(): value_window[partner]  20.3 us
    while x32, local copies, waits for them, and re-layouts  16.5 us
    dot_general x18, matrix products, convolve(): jnp.dot(window.reshape(-1, channels), kernel[row_tap, col_tap], preferred...  9.67 us
  transfers between devices with their start and end apart: 7, of which 6 were waited for; matrix products, arithmetic and copies ran while one was open for 1% of the time, Pallas kernels for 0%

profile of v1, /device:TPU:6, one launch (start us, length us, event | category | flops | bytes accessed | tf_op | source)
XLA Modules:
  0.0 319.7 jit_solution(17188495679478864343)
XLA Ops:
  0.0 2.3 fusion.19
  2.3 1.9 collective-permute-start
  4.3 8.0 %collective-permute-start.1 = (bf16[1,512,128]{2,1,0:T(8,128)(2,1)S(1)}, bf16[1,512,128]{2,1,0:T(8,128)(2,1)S(1)}, u32[]{:S(2)}, u32[]{:S(2)}) collective-permute-start(bf16[1,512,128]{2,1,0:T(8,128)(2,1)S(1)} %get-tuple-element.79), channel_id=1, source_target_pairs={{1,0},{2,1},{3,2},{4,3},{5,4},{6,5},{7,6},{8,7},{9,8},{10,9},{11,1... | collective-permute-start | bytes 393224 | tf_op jit(solution)/shard_map/ppermute | solution.py:20
  13.0 1.8 collective-permute-done.1
  19.5 1.9 collective-permute-start.2
  21.5 7.4 %collective-permute-start.3 = (bf16[1,512,128]{2,1,0:T(8,128)(2,1)S(1)}, bf16[1,512,128]{2,1,0:T(8,128)(2,1)S(1)}, u32[]{:S(2)}, u32[]{:S(2)}) collective-permute-start(bf16[1,512,128]{2,1,0:T(8,128)(2,1)S(1)} %get-tuple-element.77), channel_id=1, source_target_pairs={{1,0},{2,1},{3,2},{4,3},{5,4},{6,5},{7,6},{8,7},{9,8},{10,9},{11,1... | collective-permute-start | bytes 393224 | tf_op jit(solution)/shard_map/ppermute | solution.py:20
  29.6 1.8 collective-permute-done.3
  38.1 5.4 %stack.3 = bf16[8,1,8,512,128]{4,3,2,1,0:T(8,128)(2,1)} broadcast(bf16[8,512,128]{2,1,0:T(8,128)(2,1)S(1)} %multiply_convert_fusion), dimensions={2,3,4} | broadcast | bytes 9437184 | tf_op jit(solution)/shard_map/stack | solution.py:53
  43.5 6.0 %all-to-all-start = ((bf16[8,1,8,512,128]{4,3,2,1,0:T(8,128)(2,1)}), bf16[8,1,8,512,128]{4,3,2,1,0:T(8,128)(2,1)}, u32[]{:S(2)}, u32[]{:S(2)}) async-start(bf16[8,1,8,512,128]{4,3,2,1,0:T(8,128)(2,1)} %stack.3), calls=%async_computation | async-start | bytes 16777216 | tf_op jit(solution)/shard_map/all_to_all | solution.py:53
  49.8 87.7 %all-to-all-done = bf16[8,1,8,512,128]{4,3,2,1,0:T(8,128)(2,1)} async-done(((bf16[8,1,8,512,128]{4,3,2,1,0:T(8,128)(2,1)}), bf16[8,1,8,512,128]{4,3,2,1,0:T(8,128)(2,1)}, u32[]{:S(2)}, u32[]{:S(2)}) %all-to-all-start) | async-done | bytes 8388640 | tf_op jit(solution)/shard_map/all_to_all | solution.py:53
  137.4 4.3 %gather_fusion = bf16[2,8,512,128]{3,2,1,0:T(8,128)(2,1)S(1)} fusion(bf16[8,8,512,128]{3,2,1,0:T(8,128)(2,1)} %bitcast.48, s32[1024]{0:T(1024)S(1)} %pad_clamp_fusion), kind=kCustom, calls=%fused_computation | custom fusion | bytes 4194312 | tf_op jit(solution)/shard_map/jit(_take)/gather | solution.py:56
  142.1 1.9 collective-permute-start.4
  144.0 8.5 %collective-permute-start.5 = (bf16[2,1,512,128]{3,2,1,0:T(8,128)(2,1)S(1)}, bf16[2,1,512,128]{3,2,1,0:T(8,128)(2,1)S(1)}, u32[]{:S(2)}, u32[]{:S(2)}) collective-permute-start(bf16[2,1,512,128]{3,2,1,0:T(8,128)(2,1)S(1)} %get-tuple-element.75), channel_id=1, source_target_pairs={{1,0},{2,1},{3,2},{4,3},{5,4},{6,5},{7,6},{8,7},{9,8},{10,9},{11,1... | collective-permute-start | bytes 786440 | tf_op jit(solution)/shard_map/ppermute | solution.py:20
  154.7 1.8 collective-permute-done.5
  156.8 2.3 convolution_convert_fusion.1
  159.1 2.3 convolution_convert_fusion
  161.5 152.9 %while.10 = (s32[]{:T(128)}, f32[8,512,128]{2,1,0:T(8,128)}, s32[8]{0:T(128)S(1)}, bf16[8,512,128]{2,1,0:T(8,128)(2,1)}, bf16[2,10,512,128]{3,2,1,0:T(8,128)(2,1...) while((s32[]{:T(128)}, f32[8,512,128]{2,1,0:T(8,128)}, ...), condition=%wide.region_6.7_spmd, body=%wide.region_1.0_spmd.sunk | while | flops 850065920 | bytes 38892316 | solution.py:135
  164.1 2.5 constant_dynamic-slice_fusion.5
  168.8 1.7 fusion.149
  171.5 1.6 fusion.146
  173.1 1.6 copy-done.2
  175.3 2.8 fusion.148
  178.0 2.5 fusion.151
  183.2 2.5 constant_dynamic-slice_fusion.5
  187.9 1.7 fusion.149
  192.2 1.6 copy-done.2
  194.4 2.8 fusion.148
  197.1 2.5 fusion.151
  202.3 2.5 constant_dynamic-slice_fusion.5
  207.0 1.7 fusion.149
  209.7 1.6 fusion.146
  211.3 1.6 copy-done.2
  213.5 2.8 fusion.148
  216.2 2.5 fusion.151
  221.5 2.5 constant_dynamic-slice_fusion.5
  226.1 1.7 fusion.149
  228.8 1.6 fusion.146
  230.4 1.6 copy-done.2
  232.6 2.8 fusion.148
  235.3 2.5 fusion.151
  240.6 2.5 constant_dynamic-slice_fusion.5
  245.2 1.7 fusion.149
  247.9 1.6 fusion.146
  249.5 1.6 copy-done.2
  251.7 2.8 fusion.148
  254.5 2.5 fusion.151
  259.7 2.5 constant_dynamic-slice_fusion.5
  264.3 1.7 fusion.149
  268.6 1.6 copy-done.2
  270.8 2.8 fusion.148
  273.6 2.5 fusion.151
  278.8 2.5 constant_dynamic-slice_fusion.5
  283.4 1.7 fusion.149
  286.1 1.6 fusion.146
  287.7 1.6 copy-done.2
  289.9 2.8 fusion.148
  292.7 2.5 fusion.151
  297.9 2.5 constant_dynamic-slice_fusion.5
  302.5 1.7 fusion.149
  306.8 1.6 copy-done.2
  309.0 2.8 fusion.148
  311.8 2.5 fusion.151
  314.3 2.4 multiply_reduce_fusion
  316.7 2.9 add_bitcast_fusion
  (123 shorter events, 43.9 us)
Async XLA Ops:
  0.0 156.8 %copy-start = (bf16[128,128]{1,0:T(8,128)(2,1)S(1)}, bf16[128,128]{1,0:T(8,128)(2,1)}, u32[]{:S(2)}) copy-start(bf16[128,128]{1,0:T(8,128)(2,1)} %param.19) | copy-start | bytes 98308
  0.0 12.3 %copy-start.6 = (f32[1,8,512,128]{3,2,1,0:T(8,128)S(1)}, f32[1,8,512,128]{3,2,1,0:T(8,128)}, u32[]{:S(2)}) copy-start(f32[1,8,512,128]{3,2,1,0:T(8,128)} %param.13) | copy-start | bytes 6291460
  0.0 12.3 %copy-start.8 = (bf16[3,3,128,128]{3,2,1,0:T(8,128)(2,1)S(1)}, bf16[3,3,128,128]{3,2,1,0:T(8,128)(2,1)}, u32[]{:S(2)}) copy-start(bf16[3,3,128,128]{3,2,1,0:T(8,128)(2,1)} %param.16) | copy-start | bytes 884740
  2.3 10.7 %collective-permute-start = (bf16[1,512,128]{2,1,0:T(8,128)(2,1)S(1)}, bf16[1,512,128]{2,1,0:T(8,128)(2,1)S(1)}, u32[]{:S(2)}, u32[]{:S(2)}) collective-permute-start(bf16[1,512,128]{2,1,0:T(8,128)(2,1)S(1)} %get-tuple-element.78), channel_id=1, source_target_pairs={{0,1},{1,2},{2,3},{3,4},{4,5},{5,6},{6,7},{7,8},{8,9},{9,10},{10,1... | collective-permute-start | bytes 393224 | tf_op jit(solution)/shard_map/ppermute | solution.py:18
  4.3 10.6 %collective-permute-start.1 = (bf16[1,512,128]{2,1,0:T(8,128)(2,1)S(1)}, bf16[1,512,128]{2,1,0:T(8,128)(2,1)S(1)}, u32[]{:S(2)}, u32[]{:S(2)}) collective-permute-start(bf16[1,512,128]{2,1,0:T(8,128)(2,1)S(1)} %get-tuple-element.79), channel_id=1, source_target_pairs={{1,0},{2,1},{3,2},{4,3},{5,4},{6,5},{7,6},{8,7},{9,8},{10,9},{11,1... | collective-permute-start | bytes 393224 | tf_op jit(solution)/shard_map/ppermute | solution.py:20
  18.1 10.8 %copy-start.7 = (bf16[3,3,128,128]{3,2,1,0:T(8,128)(2,1)S(1)}, bf16[3,3,128,128]{3,2,1,0:T(8,128)(2,1)}, u32[]{:S(2)}) copy-start(bf16[3,3,128,128]{3,2,1,0:T(8,128)(2,1)} %param.17) | copy-start | bytes 884740
  19.5 10.1 %collective-permute-start.2 = (bf16[1,512,128]{2,1,0:T(8,128)(2,1)S(1)}, bf16[1,512,128]{2,1,0:T(8,128)(2,1)S(1)}, u32[]{:S(2)}, u32[]{:S(2)}) collective-permute-start(bf16[1,512,128]{2,1,0:T(8,128)(2,1)S(1)} %get-tuple-element.76), channel_id=1, source_target_pairs={{0,1},{1,2},{2,3},{3,4},{4,5},{5,6},{6,7},{7,8},{8,9},{9,10},{10,1... | collective-permute-start | bytes 393224 | tf_op jit(solution)/shard_map/ppermute | solution.py:18
  21.5 9.9 %collective-permute-start.3 = (bf16[1,512,128]{2,1,0:T(8,128)(2,1)S(1)}, bf16[1,512,128]{2,1,0:T(8,128)(2,1)S(1)}, u32[]{:S(2)}, u32[]{:S(2)}) collective-permute-start(bf16[1,512,128]{2,1,0:T(8,128)(2,1)S(1)} %get-tuple-element.77), channel_id=1, source_target_pairs={{1,0},{2,1},{3,2},{4,3},{5,4},{6,5},{7,6},{8,7},{9,8},{10,9},{11,1... | collective-permute-start | bytes 393224 | tf_op jit(solution)/shard_map/ppermute | solution.py:20
  34.7 2.6 copy-start.13
  36.0 1.3 copy-start.4
  43.5 6.0 %copy-start.11 = (s32[8,2]{0,1:T(2,128)S(1)}, s32[8,2]{0,1:T(2,128)}, u32[]{:S(2)}) copy-start(s32[8,2]{0,1:T(2,128)} %param.15) | copy-start | bytes 196
  43.5 93.9 %all-to-all-start = ((bf16[8,1,8,512,128]{4,3,2,1,0:T(8,128)(2,1)}), bf16[8,1,8,512,128]{4,3,2,1,0:T(8,128)(2,1)}, u32[]{:S(2)}, u32[]{:S(2)}) async-start(bf16[8,1,8,512,128]{4,3,2,1,0:T(8,128)(2,1)} %stack.3), calls=%async_computation | async-start | bytes 16777216 | tf_op jit(solution)/shard_map/all_to_all | solution.py:53
  141.8 10.8 %copy-start.9 = (bf16[128,128]{1,0:T(8,128)(2,1)S(1)}, bf16[128,128]{1,0:T(8,128)(2,1)}, u32[]{:S(2)}) copy-start(bf16[128,128]{1,0:T(8,128)(2,1)} %param.18) | copy-start | bytes 98308
  142.1 12.6 %collective-permute-start.4 = (bf16[2,1,512,128]{3,2,1,0:T(8,128)(2,1)S(1)}, bf16[2,1,512,128]{3,2,1,0:T(8,128)(2,1)S(1)}, u32[]{:S(2)}, u32[]{:S(2)}) collective-permute-start(bf16[2,1,512,128]{3,2,1,0:T(8,128)(2,1)S(1)} %get-tuple-element.74), channel_id=1, source_target_pairs={{0,1},{1,2},{2,3},{3,4},{4,5},{5,6},{6,7},{7,8},{8,9},{9,10},{10,1... | collective-permute-start | bytes 786440 | tf_op jit(solution)/shard_map/ppermute | solution.py:18
  144.0 12.4 %collective-permute-start.5 = (bf16[2,1,512,128]{3,2,1,0:T(8,128)(2,1)S(1)}, bf16[2,1,512,128]{3,2,1,0:T(8,128)(2,1)S(1)}, u32[]{:S(2)}, u32[]{:S(2)}) collective-permute-start(bf16[2,1,512,128]{3,2,1,0:T(8,128)(2,1)S(1)} %get-tuple-element.75), channel_id=1, source_target_pairs={{1,0},{2,1},{3,2},{4,3},{5,4},{6,5},{7,6},{8,7},{9,8},{10,9},{11,1... | collective-permute-start | bytes 786440 | tf_op jit(solution)/shard_map/ppermute | solution.py:20
  156.8 2.4 copy-start.10
  159.1 2.3 copy-start.14
  170.5 1.0 copy-start.3
  173.1 1.6 copy-start.2
  189.6 1.0 copy-start.3
  192.2 1.6 copy-start.2
  208.7 1.0 copy-start.3
  211.3 1.6 copy-start.2
  227.8 1.0 copy-start.3
  230.4 1.6 copy-start.2
  246.9 1.0 copy-start.3
  249.5 1.6 copy-start.2
  266.0 1.0 copy-start.3
  268.6 1.6 copy-start.2
  285.1 1.0 copy-start.3
  287.7 1.6 copy-start.2
  304.2 1.0 copy-start.3
  306.8 1.6 copy-start.2
  314.3 2.4 copy-start.5
  314.3 2.4 copy-start.12
  316.7 3.0 copy-start.1
